TPU v7x, 256 devices: a whole 4x4x8 slice. The times are simulated.
256 devices in a mesh: seq: 32 (over z_hi, x, core), tensor: 8 (over y, z_lo).
Axes of the slice: x: 4, y: 4, z: 8 (z_hi: 4, z_lo: 2; z = z_hi * 2 + z_lo), core: 2. Of those that a mesh axis runs over, the one named last changes fastest.
Arguments:
- tokens: bfloat16 [4096, 2048], P('seq'), may hold values from -6 to 6
- lengths: int32 [8], replicated, may hold values from 1 to 2048, 4096 in all
- page_table: int32 [256], replicated, may hold values from 0 to 255, each once
- attention_gain: float32 [2048], replicated, may hold values from 0.25 to 1.75
- query_weight: bfloat16 [2048, 2048], P(None, 'tensor')
- key_weight: bfloat16 [2048, 2048], P(None, 'tensor')
- value_weight: bfloat16 [2048, 2048], P(None, 'tensor'), may hold values from -0.125 to 0.125
- out_weight: bfloat16 [2048, 2048], P('tensor'), may hold values from -0.125 to 0.125
- expert_gain: float32 [2048], replicated, may hold values from 0.25 to 1.75
- router_weight: bfloat16 [2048, 64], replicated, may hold values from -0.03125 to 0.03125
- expert_ids: int32 [4096, 8], P('seq'), may hold values from 0 to 63, all different within a row; in each aligned block of 128 rows (0 to 127, 128 to 255, ...) at most 24 rows name the same one
- gate_weight: bfloat16 [64, 2048, 1024], P('seq', None, 'tensor'), may hold values from -0.125 to 0.125
- up_weight: bfloat16 [64, 2048, 1024], P('seq', None, 'tensor'), may hold values from -0.125 to 0.125
- down_weight: bfloat16 [64, 1024, 2048], P('seq', 'tensor'), may hold values from -6 to 6
Outputs:
- layer_out: bfloat16 [4096, 2048], P('seq')
- key_cache: bfloat16 [256, 16, 2048], P('seq', None, 'tensor')
- value_cache: bfloat16 [256, 16, 2048], P('seq', None, 'tensor')
Inputs may be any that keep to these rules, and one draw needn't show every extreme that they name: The 8 lengths sum to 4096; the longest is exactly 2048. `page_table`: every page number appears once. `expert_ids`: each token names 8 different experts; among the 128 tokens of one index of seq no expert is named more than 24 times, a bound that some block reaches.
All inputs are finite; a program needn't handle non-finite values.
Results may differ from a plain program's by a relative error of at most 0.023.
Values may be sent and summed in bfloat16 or wider, within the bound.
A program may use at most 128 MiB of HBM per device.

v0:
```python
import jax
import jax.numpy as jnp
from jax import lax
from jax.sharding import PartitionSpec as P

HEAD_DIM = 128
PAGE = 16
epsilon = 1e-05
rope_base = 10000.0


def rms_scale(matrix, scaling):
    mean_square = jnp.mean(matrix * matrix, axis=-1, keepdims=True)
    return matrix * lax.rsqrt(mean_square + epsilon) * scaling


def segment_info(lengths, places):
    starts = jnp.cumsum(lengths) - lengths
    inside = (places[:, None] >= starts[None, :]).astype(jnp.int32)
    segment = jnp.sum(inside, axis=1) - 1
    slot_ids = jnp.arange(starts.shape[0], dtype=jnp.int32)
    seg_start = jnp.sum(
        jnp.where(slot_ids[None, :] == segment[:, None], starts[None, :], 0), axis=1
    )
    return (segment, places - seg_start)


def rotate(matrix, position):
    half_dim = matrix.shape[-1] // 2
    frequency = jnp.exp(
        -jnp.log(rope_base) * jnp.arange(half_dim, dtype=jnp.float32) * (2.0 / matrix.shape[-1])
    )
    angles = position.astype(jnp.float32)[:, None] * frequency[None, :]
    cosine = jnp.cos(angles)[:, None, :]
    sine_part = jnp.sin(angles)[:, None, :]
    first_half = matrix[..., :half_dim]
    second = matrix[..., half_dim:]
    return jnp.concatenate(
        [first_half * cosine - second * sine_part, second * cosine + first_half * sine_part],
        axis=-1,
    )


def local(
    tokens,
    lengths,
    page_table,
    attention_gain,
    query_weight,
    key_weight,
    value_weight,
    out_weight,
    expert_gain,
    router_weight,
    expert_ids,
    gate_weight,
    up_weight,
    down_weight,
):
    row_count = tokens.shape[0]
    feature_count = tokens.shape[1]
    span_size = query_weight.shape[1]
    head_count = span_size // HEAD_DIM
    shard_id = lax.axis_index("seq")
    places = shard_id * row_count + jnp.arange(row_count, dtype=jnp.int32)
    segment, position = segment_info(lengths, places)
    stream = tokens.astype(jnp.float32)
    normed = rms_scale(stream, attention_gain).astype(jnp.bfloat16)
    queries = rotate(
        jnp.dot(normed, query_weight, preferred_element_type=jnp.float32).reshape(
            row_count, head_count, HEAD_DIM
        ),
        position,
    ).astype(jnp.bfloat16)
    key_rows = (
        rotate(
            jnp.dot(normed, key_weight, preferred_element_type=jnp.float32).reshape(
                row_count, head_count, HEAD_DIM
            ),
            position,
        )
        .astype(jnp.bfloat16)
        .reshape(row_count, span_size)
    )
    value_rows = jnp.dot(normed, value_weight, preferred_element_type=jnp.float32).astype(
        jnp.bfloat16
    )
    page_rows = row_count // PAGE
    my_pages = shard_id * page_rows + jnp.arange(page_rows, dtype=jnp.int32)
    owned = (page_table[None, :] == my_pages[:, None]).astype(jnp.bfloat16)
    score_scale = HEAD_DIM ** (-0.5)
    state = (
        jnp.full((head_count, row_count), -1e30, jnp.float32),
        jnp.zeros((head_count, row_count), jnp.float32),
        jnp.zeros((head_count, row_count, HEAD_DIM), jnp.float32),
    )
    key_piece = lax.all_gather(key_rows, "seq", axis=0, tiled=True)
    value_piece = lax.all_gather(value_rows, "seq", axis=0, tiled=True)
    piece_rows = key_piece.shape[0]
    key_pages = jnp.dot(
        owned,
        key_piece.reshape(piece_rows // PAGE, PAGE * span_size),
        preferred_element_type=jnp.float32,
    )
    value_pages = jnp.dot(
        owned,
        value_piece.reshape(piece_rows // PAGE, PAGE * span_size),
        preferred_element_type=jnp.float32,
    )
    row_peak, row_total, weighted = state
    piece_rows = key_piece.shape[0]
    key_places = jnp.arange(piece_rows, dtype=jnp.int32)
    key_segments, _ = segment_info(lengths, key_places)
    scores = (
        jnp.einsum(
            "qhd,khd->hqk",
            queries,
            key_piece.reshape(piece_rows, head_count, HEAD_DIM),
            preferred_element_type=jnp.float32,
        )
        * score_scale
    )
    allowed = (
        (segment[:, None] == key_segments[None, :]) & (key_places[None, :] <= places[:, None])
    )[None]
    new_peak = jnp.maximum(row_peak, jnp.max(jnp.where(allowed, scores, -1e30), axis=-1))
    raised = jnp.where(allowed, jnp.exp(scores - new_peak[:, :, None]), 0.0)
    row_total = jnp.sum(raised, axis=-1)
    weighted = jnp.einsum(
        "hqk,khd->hqd",
        raised.astype(jnp.bfloat16),
        value_piece.reshape(piece_rows, head_count, HEAD_DIM),
        preferred_element_type=jnp.float32,
    )
    state = (new_peak, row_total, weighted)
    state, key_pages, value_pages = (state, key_pages, value_pages)
    _, row_total, weighted = state
    attended = (
        jnp.transpose(weighted / row_total[:, :, None], (1, 0, 2))
        .reshape(row_count, span_size)
        .astype(jnp.bfloat16)
    )
    head_part = jnp.dot(attended, out_weight, preferred_element_type=jnp.float32)
    hidden = stream + lax.psum(head_part.astype(jnp.bfloat16), "tensor").astype(jnp.float32)
    moe_input = rms_scale(hidden, expert_gain).astype(jnp.bfloat16)
    expert_count = router_weight.shape[1]
    probability = jax.nn.softmax(
        jnp.dot(moe_input, router_weight, preferred_element_type=jnp.float32), axis=-1
    )
    expert_range = jnp.arange(expert_count, dtype=jnp.int32)
    chosen = jnp.sum(
        jnp.where(
            expert_ids[:, :, None] == expert_range[None, None, :], probability[:, None, :], 0.0
        ),
        axis=-1,
    )
    top_count = expert_ids.shape[1]
    flat_ids = expert_ids.reshape(-1)
    onehot = (flat_ids[:, None] == expert_range[None, :]).astype(jnp.int32)
    slot_rank = jnp.sum(jnp.cumsum(onehot, axis=0) * onehot, axis=1) - 1
    members = lax.axis_size("tensor")
    sources = lax.axis_size("seq")
    local_count = gate_weight.shape[0]
    base_room = row_count * top_count * 3 // (2 * expert_count)
    capacity = members * ((base_room + members - 1) // members)
    owners = jnp.arange(row_count * top_count, dtype=jnp.int32) // top_count
    slot_index = flat_ids * capacity + slot_rank
    row_table = (
        jnp.full((expert_count * capacity,), row_count, jnp.int32).at[slot_index].set(owners)
    )
    padded = jnp.concatenate([moe_input, jnp.zeros((1, feature_count), jnp.bfloat16)], axis=0)
    outgoing = padded[row_table].reshape(sources, local_count, capacity, feature_count)
    arrived = lax.all_to_all(outgoing, "seq", split_axis=0, concat_axis=0, tiled=True)
    gate_out = jnp.einsum(
        "sjnd,jdf->sjnf", arrived, gate_weight, preferred_element_type=jnp.float32
    )
    up_out = jnp.einsum("sjnd,jdf->sjnf", arrived, up_weight, preferred_element_type=jnp.float32)
    activation = (jax.nn.silu(gate_out) * up_out).astype(jnp.bfloat16)
    returned = lax.all_to_all(
        jnp.einsum(
            "sjnf,jfd->sjnd", activation, down_weight, preferred_element_type=jnp.float32
        ).astype(jnp.bfloat16),
        "seq",
        split_axis=0,
        concat_axis=0,
        tiled=True,
    )
    flat_rows = returned.reshape(expert_count * capacity, feature_count)
    picked = flat_rows[slot_index].astype(jnp.float32)
    mixture_part = jnp.sum(
        picked.reshape(row_count, top_count, feature_count) * chosen[:, :, None], axis=1
    )
    mixture = lax.psum(mixture_part.astype(jnp.bfloat16), "tensor").astype(jnp.float32)
    layer_out = (hidden + mixture).astype(jnp.bfloat16)
    key_cache = key_pages.reshape(page_rows, PAGE, span_size).astype(jnp.bfloat16)
    value_cache = value_pages.reshape(page_rows, PAGE, span_size).astype(jnp.bfloat16)
    return (layer_out, key_cache, value_cache)


def solution(mesh):
    return jax.shard_map(
        local,
        mesh=mesh,
        in_specs=(
            P("seq", None),
            P(),
            P(),
            P(),
            P(None, "tensor"),
            P(None, "tensor"),
            P(None, "tensor"),
            P("tensor", None),
            P(),
            P(),
            P("seq", None),
            P("seq", None, "tensor"),
            P("seq", None, "tensor"),
            P("seq", "tensor", None),
        ),
        out_specs=(P("seq", None), P("seq", None, "tensor"), P("seq", None, "tensor")),
        check_vma=False,
    )
```

profile of v0, /device:TPU:2, one launch (start us, length us, event | category | flops | bytes accessed | tf_op | source)
XLA Modules:
  0.0 651.1 jit_solution(417091453030510193)
XLA Ops:
  10.3 1.8 fusion.75
  12.2 1.8 fusion.77
  15.7 2.2 convolution_convert_fusion.3
  18.5 18.0 %reduce-window.20 = s32[64,8,128]{2,1,0:T(8,128)S(1)} reduce-window(s32[64,8,128]{2,1,0:T(8,128)S(1)} %fusion.52, s32[]{:T(128)} %constant.30.clone.1), window={size=1x1x128 pad=0_0x0_0x127_0}, to_apply=%region_9.10 | reduce-window | flops 8323072 | bytes 524292 | tf_op jit(solution)/shard_map/reduce-window.1
  37.8 35.6 %all-gather.3.cloned.1.call-done = bf16[4096,256]{0,1:T(8,128)(2,1)} async-done(((bf16[128,256]{0,1:T(8,128)(2,1)}), bf16[4096,256]{0,1:T(8,128)(2,1)}) %all-gather.3.cloned.1.call-update) | async-done | bytes 2097168 | tf_op jit(solution)/shard_map/all_gather | solution.py:97
  73.4 2.9 select_reduce_fusion
  76.3 1.9 copy-done.2
  79.3 49.4 %all-gather.5.cloned.1.call-done = bf16[4096,256]{1,0:T(8,128)(2,1)} async-done(((bf16[128,256]{1,0:T(8,128)(2,1)}), bf16[4096,256]{1,0:T(8,128)(2,1)}) %all-gather.5.cloned.1.call-update) | async-done | bytes 2097168 | tf_op jit(solution)/shard_map/all_gather | solution.py:98
  128.7 4.1 copy.95
  132.8 3.9 fusion.31
  137.9 4.3 scatter_custom_fusion
  142.3 74.3 %all-reduce.4.cloned.1.call-done = bf16[128,2048]{1,0:T(8,128)(2,1)} async-done(((bf16[128,2048]{1,0:T(8,128)(2,1)}), bf16[128,2048]{1,0:T(8,128)(2,1)}) %all-reduce.4.cloned.1.call-update) | async-done | bytes 524304 | tf_op jit(solution)/shard_map/psum | solution.py:144
  216.6 1.3 multiply_reduce_fusion
  217.9 1.3 multiply_convert_fusion
  220.0 7.1 %gather_fusion = bf16[1536,2048]{1,0:T(8,128)(2,1)} fusion(bf16[129,2048]{1,0:T(8,128)(2,1)S(1)} %concatenate.13, s32[2048]{0:T(1024)S(1)} %pad_clamp_fusion), kind=kCustom, calls=%fused_computation | custom fusion | bytes 12589056 | tf_op jit(solution)/shard_map/gather | solution.py:172
  227.1 149.0 %all_to_all.10 = bf16[32,2,24,2048]{3,2,1,0:T(8,128)(2,1)S(1)} all-to-all(bf16[32,2,24,2048]{3,2,1,0:T(8,128)(2,1)} %bitcast.85), channel_id=1, replica_groups=mesh['seq'=32,'tensor'=8] {'seq'}, dimensions={0} | all-to-all | bytes 12582912 | tf_op jit(solution)/shard_map/all_to_all | solution.py:173
  376.1 2.7 copy-done.5
  378.8 1.9 fusion.13
  380.7 8.9 %convert_bitcast_fusion = bf16[32,2,24,2048]{3,2,0,1:T(8,128)(2,1)} fusion(bf16[2,128,2048]{2,1,0:T(8,128)(2,1)S(1)} %copy-done, bf16[32,2,24,2048]{3,2,1,0:T(8,128)(2,1)} %copy-done.5, bf16[2,2048,128]{2,1,0:T(8,128)(2,1)S(1)} %copy-done.14, f32[32,2,24,128]{3,2,0,1:T(8,128)S(1)} %fusion.13), kind=kOutput, calls=%fused_computation.5 | convolution fusion | flops 1614938112 | bytes 15466496 | tf_op jit(solution)/shard_map/sjnf,jfd->sjnd/dot_general | solution.py:180
  389.6 6.6 %copy.84 = bf16[32,2,24,2048]{3,2,1,0:T(8,128)(2,1)} copy(bf16[32,2,24,2048]{3,2,0,1:T(8,128)(2,1)} %convert_bitcast_fusion) | data formatting | bytes 12582912 | tf_op jit(solution)/shard_map/convert_element_type | solution.py:182
  396.2 6.6 %all-to-all-start.1 = ((bf16[32,2,24,2048]{3,2,1,0:T(8,128)(2,1)}), bf16[32,2,24,2048]{3,2,1,0:T(8,128)(2,1)}, u32[]{:S(2)}, u32[]{:S(2)}) async-start(bf16[32,2,24,2048]{3,2,1,0:T(8,128)(2,1)} %copy.84), calls=%async_computation.1 | async-start | bytes 12582912 | tf_op jit(solution)/shard_map/all_to_all | solution.py:179
  403.1 3.3 copy.86
  406.4 2.4 reshape.277
  408.8 4.1 copy.87
  413.4 130.8 %all-to-all-done.1 = bf16[32,2,24,2048]{3,2,1,0:T(8,128)(2,1)} async-done(((bf16[32,2,24,2048]{3,2,1,0:T(8,128)(2,1)}), bf16[32,2,24,2048]{3,2,1,0:T(8,128)(2,1)}, u32[]{:S(2)}, u32[]{:S(2)}) %all-to-all-start.1) | async-done | bytes 6291488 | tf_op jit(solution)/shard_map/all_to_all | solution.py:179
  544.2 12.4 %gather_fusion.1 = bf16[1024,2048]{1,0:T(8,128)(2,1)} fusion(bf16[1536,2048]{1,0:T(8,128)(2,1)} %bitcast.22, s32[1024]{0:T(1024)S(1)} %broadcast_clamp_fusion), kind=kCustom, calls=%fused_computation.1 | custom fusion | bytes 8392704 | tf_op jit(solution)/shard_map/gather | solution.py:189
  556.6 7.5 %fusion = bf16[128,2048]{1,0:T(8,128)(2,1)} fusion(bf16[1024,2048]{1,0:T(8,128)(2,1)} %gather_fusion.1, f32[128,8]{1,0:T(8,128)S(1)} %copy.85), kind=kLoop, calls=%fused_computation.4 | loop fusion | flops 6029312 | bytes 4722688 | tf_op jit(solution)/shard_map/reduce_sum | solution.py:190
  564.1 2.2 convolution_convert_fusion.2
  567.0 2.4 reshape.278
  569.4 3.4 copy.88
  574.0 68.2 %all-reduce.6.cloned.1.call-done = bf16[128,2048]{1,0:T(8,128)(2,1)} async-done(((bf16[128,2048]{1,0:T(8,128)(2,1)}), bf16[128,2048]{1,0:T(8,128)(2,1)}) %all-reduce.6.cloned.1.call-update) | async-done | bytes 524304 | tf_op jit(solution)/shard_map/psum | solution.py:193
  642.2 2.4 add_convert_fusion
  (92 shorter events, 12.5 us)
Async XLA Ops:
  7.2 373.5 %copy-start = (bf16[2,128,2048]{2,1,0:T(8,128)(2,1)S(1)}, bf16[2,128,2048]{2,1,0:T(8,128)(2,1)}, u32[]{:S(2)}) copy-start(bf16[2,128,2048]{2,1,0:T(8,128)(2,1)} %param.27) | copy-start | bytes 3145732
  7.2 8.5 %copy-start.4 = (bf16[128,2048]{1,0:T(8,128)(2,1)S(1)}, bf16[128,2048]{1,0:T(8,128)(2,1)}, u32[]{:S(2)}) copy-start(bf16[128,2048]{1,0:T(8,128)(2,1)} %param.14) | copy-start | bytes 1572868
  7.2 8.5 %copy-start.15 = (f32[2048]{0:T(1024)S(1)}, f32[2048]{0:T(1024)}, u32[]{:S(2)}) copy-start(f32[2048]{0:T(1024)} %param.17) | copy-start | bytes 24580
  7.2 66.1 %all-gather.3.cloned.1.call-start = ((), (), s32[]{:S(2)}) async-start(), calls=%async_computation.2 | async-start | bytes 2162688 | tf_op jit(solution)/shard_map/all_gather | solution.py:97
  10.3 7.7 %copy-start.10 = (s32[128,8]{0,1:T(8,128)S(1)}, s32[128,8]{0,1:T(8,128)}, u32[]{:S(2)}) copy-start(s32[128,8]{0,1:T(8,128)} %param.24) | copy-start | bytes 12292
  15.6 113.1 %all-gather.5.cloned.1.call-start = ((), (), s32[]{:S(2)}) async-start(), calls=%async_computation.3 | async-start | bytes 2162688 | tf_op jit(solution)/shard_map/all_gather | solution.py:98
  17.9 198.7 %all-reduce.4.cloned.1.call-start = ((), (), s32[]{:S(2)}) async-start(), calls=%async_computation.4 | async-start | bytes 1048576 | tf_op jit(solution)/shard_map/psum | solution.py:144
  76.3 1.9 copy-start.2
  132.8 4.0 copy-start.8
  132.8 85.1 %copy-start.11 = (f32[2048]{0:T(1024)S(1)}, f32[2048]{0:T(1024)}, u32[]{:S(2)}) copy-start(f32[2048]{0:T(1024)} %param.22) | copy-start | bytes 24580
  219.2 0.8 copy-start.6
  227.1 151.7 %copy-start.13 = (bf16[2,2048,128]{2,1,0:T(8,128)(2,1)S(1)}, bf16[2,2048,128]{2,1,0:T(8,128)(2,1)}, u32[]{:S(2)}) copy-start(bf16[2,2048,128]{2,1,0:T(8,128)(2,1)} %param.25) | copy-start | bytes 3145732
  376.1 2.7 copy-start.5
  378.8 1.9 copy-start.14
  396.2 148.0 %all-to-all-start.1 = ((bf16[32,2,24,2048]{3,2,1,0:T(8,128)(2,1)}), bf16[32,2,24,2048]{3,2,1,0:T(8,128)(2,1)}, u32[]{:S(2)}, u32[]{:S(2)}) async-start(bf16[32,2,24,2048]{3,2,1,0:T(8,128)(2,1)} %copy.84), calls=%async_computation.1 | async-start | bytes 12582912 | tf_op jit(solution)/shard_map/all_to_all | solution.py:179
  402.8 239.4 %all-reduce.6.cloned.1.call-start = ((), (), s32[]{:S(2)}) async-start(), calls=%async_computation.5 | async-start | bytes 1048576 | tf_op jit(solution)/shard_map/psum | solution.py:193
  406.3 6.5 copy-start.7
  406.4 6.5 copy-start.9
  556.6 7.5 %copy-start.12 = (s32[256]{0:T(256)S(1)}, s32[256]{0:T(256)}, u32[]{:S(2)}) copy-start(s32[256]{0:T(256)} %param.16) | copy-start | bytes 3076
  556.6 10.4 %copy-start.3 = (bf16[4096,256]{1,0:T(8,128)(2,1)S(1)}, bf16[4096,256]{1,0:T(8,128)(2,1)}, u32[]{:S(2)}) copy-start(bf16[4096,256]{1,0:T(8,128)(2,1)} %all-gather.5.cloned.1.call-done) | copy-start | bytes 6291460
  569.3 75.2 %copy-start.1 = (bf16[2,128,2048]{2,1,0:T(8,128)(2,1)S(1)}, bf16[2,128,2048]{2,1,0:T(8,128)(2,1)}, u32[]{:S(2)}) copy-start(bf16[2,128,2048]{2,1,0:T(8,128)(2,1)} %param.27) | copy-start | bytes 3145732
Sparse Core Ops, SparseCore 0:
  15.7 57.5 all-gather.2
  76.5 52.1 all-gather.4
  138.0 78.5 all-reduce.3
  564.2 77.9 all-reduce.5
where the time goes:
time: 652 us; the launch traced here: 651 us
  waiting for transfers between devices  358 us (55%)
  blocking collectives  149 us (23%)
  local copies, waits for them, and re-layouts  58.9 us (9%)
  other arithmetic  36 us (6%)
  matrix products  27.7 us (4%)
  between operations  14.2 us (2%)
  starting transfers between devices  6.95 us (1%)
    all_to_all x1, blocking collectives, local(): lax.all_to_all(outgoing, 'seq', split_axis=0, concat_axis=0, tiled=True)  149 us
    all_to_all x1, waiting for transfers between devices, local(): lax.all_to_all(jnp.einsum('sjnf,jfd->sjnd', activation, down_weight, pref...  131 us
    psum x1, waiting for transfers between devices, local(): lax.psum(head_part.astype(jnp.bfloat16), 'tensor').astype(jnp.float32)  74.3 us
    psum x1, waiting for transfers between devices, local(): lax.psum(mixture_part.astype(jnp.bfloat16), 'tensor').astype(jnp.float32)  68.2 us
    all_gather x1, waiting for transfers between devices, local(): value_piece = lax.all_gather(value_rows, 'seq', axis=0, tiled=True)  49.4 us
    all_gather x1, waiting for transfers between devices, local(): key_piece = lax.all_gather(key_rows, 'seq', axis=0, tiled=True)  35.6 us
    another operation x5, other arithmetic  19.2 us
  transfers between devices with their start and end apart: 5, of which 5 were waited for; matrix products, arithmetic and copies ran while one was open for 8% of the time, Pallas kernels for 0%

commit v1 on v0

--- a/solution.py
+++ b/solution.py
@@ -94,8 +94,11 @@
         jnp.zeros((head_count, row_count), jnp.float32),
         jnp.zeros((head_count, row_count, HEAD_DIM), jnp.float32),
     )
-    key_piece = lax.all_gather(key_rows, "seq", axis=0, tiled=True)
-    value_piece = lax.all_gather(value_rows, "seq", axis=0, tiled=True)
+    key_piece, value_piece = jnp.split(
+        lax.all_gather(jnp.concatenate([key_rows, value_rows], axis=1), "seq", axis=0, tiled=True),
+        [key_rows.shape[1]],
+        axis=1,
+    )
     piece_rows = key_piece.shape[0]
     key_pages = jnp.dot(
         owned,

time: 652 us -> 607 us (0.931)
  waiting for transfers between devices: 358 us -> 319 us
    all_gather x2 -> x1, waiting for transfers between devices: 85 us -> 42.8 us  [local(): lax.all_gather(jnp.concatenate([key_rows, value_rows], axis=1), 'seq', ax...]
  transfers between devices with their start and end apart: 5 -> 4, of which waited for: 5 -> 4; matrix products, arithmetic and copies ran while one was open for 8% -> 7% of each run, Pallas kernels for 0% -> 0%
where the time goes in v1:
time: 607 us
  waiting for transfers between devices  319 us (53%)
  blocking collectives  149 us (25%)
  local copies, waits for them, and re-layouts  55 us (9%)
  other arithmetic  37.5 us (6%)
  matrix products  24.7 us (4%)
  between operations  14.2 us (2%)
  starting transfers between devices  7.05 us (1%)
    all_to_all x1, blocking collectives, local(): lax.all_to_all(outgoing, 'seq', split_axis=0, concat_axis=0, tiled=True)  149 us
    all_to_all x1, waiting for transfers between devices, local(): lax.all_to_all(jnp.einsum('sjnf,jfd->sjnd', activation, down_weight, pref...  133 us
    psum x1, waiting for transfers between devices, local(): lax.psum(head_part.astype(jnp.bfloat16), 'tensor').astype(jnp.float32)  73.7 us
    psum x1, waiting for transfers between devices, local(): lax.psum(mixture_part.astype(jnp.bfloat16), 'tensor').astype(jnp.float32)  69.8 us
    all_gather x1, waiting for transfers between devices, local(): lax.all_gather(jnp.concatenate([key_rows, value_rows], axis=1), 'seq', ax...  42.8 us
    another operation x5, other arithmetic  19.2 us
    gather x1, local copies, waits for them, and re-layouts, local(): picked = flat_rows[slot_index].astype(jnp.float32)  12.4 us
  transfers between devices with their start and end apart: 4, of which 4 were waited for; matrix products, arithmetic and copies ran while one was open for 7% of the time, Pallas kernels for 0%

profile of v1, /device:TPU:2, one launch (start us, length us, event | category | flops | bytes accessed | tf_op | source)
XLA Modules:
  0.0 606.5 jit_solution(626271273921527139)
XLA Ops:
  9.1 1.2 fusion.36
  10.4 1.8 convolution_convert_fusion.3
  12.1 1.8 fusion.77
  16.5 18.0 %reduce-window.20 = s32[64,8,128]{2,1,0:T(8,128)S(1)} reduce-window(s32[64,8,128]{2,1,0:T(8,128)S(1)} %fusion.54, s32[]{:T(128)} %constant.30.clone.1), window={size=1x1x128 pad=0_0x0_0x127_0}, to_apply=%region_9.10 | reduce-window | flops 8323072 | bytes 524292 | tf_op jit(solution)/shard_map/reduce-window.1
  35.3 1.3 fusion.13
  36.6 42.8 %all-gather.2.cloned.1.call-done = bf16[4096,512]{1,0:T(8,128)(2,1)} async-done(((bf16[128,512]{1,0:T(8,128)(2,1)}), bf16[4096,512]{1,0:T(8,128)(2,1)}) %all-gather.2.cloned.1.call-update) | async-done | bytes 4194320 | tf_op jit(solution)/shard_map/all_gather | solution.py:98
  79.4 4.9 fusion.81
  84.3 2.9 copy.94
  87.2 3.1 select_reduce_fusion
  92.7 1.1 convolution_convert_fusion
  93.9 4.3 scatter_custom_fusion
  98.2 73.7 %all-reduce.4.cloned.1.call-done = bf16[128,2048]{1,0:T(8,128)(2,1)} async-done(((bf16[128,2048]{1,0:T(8,128)(2,1)}), bf16[128,2048]{1,0:T(8,128)(2,1)}) %all-reduce.4.cloned.1.call-update) | async-done | bytes 524304 | tf_op jit(solution)/shard_map/psum | solution.py:147
  171.9 1.3 multiply_reduce_fusion
  173.2 1.3 multiply_convert_fusion
  175.3 7.1 %gather_fusion = bf16[1536,2048]{1,0:T(8,128)(2,1)} fusion(bf16[129,2048]{1,0:T(8,128)(2,1)S(1)} %concatenate.17, s32[2048]{0:T(1024)S(1)} %pad_clamp_fusion), kind=kCustom, calls=%fused_computation | custom fusion | bytes 12589056 | tf_op jit(solution)/shard_map/gather | solution.py:175
  182.4 149.0 %all_to_all.10 = bf16[32,2,24,2048]{3,2,1,0:T(8,128)(2,1)S(1)} all-to-all(bf16[32,2,24,2048]{3,2,1,0:T(8,128)(2,1)} %bitcast.94), channel_id=1, replica_groups=mesh['seq'=32,'tensor'=8] {'seq'}, dimensions={0} | all-to-all | bytes 12582912 | tf_op jit(solution)/shard_map/all_to_all | solution.py:176
  331.4 2.7 copy-done.7
  334.0 1.9 fusion.15
  336.0 8.9 %convert_bitcast_fusion = bf16[32,2,24,2048]{3,2,0,1:T(8,128)(2,1)} fusion(bf16[2,128,2048]{2,1,0:T(8,128)(2,1)S(1)} %copy-done, bf16[32,2,24,2048]{3,2,1,0:T(8,128)(2,1)} %copy-done.7, bf16[2,2048,128]{2,1,0:T(8,128)(2,1)S(1)} %copy-done.19, f32[32,2,24,128]{3,2,0,1:T(8,128)S(1)} %fusion.15), kind=kOutput, calls=%fused_computation.5 | convolution fusion | flops 1614938112 | bytes 15466496 | tf_op jit(solution)/shard_map/sjnf,jfd->sjnd/dot_general | solution.py:183
  344.9 6.6 %copy.85 = bf16[32,2,24,2048]{3,2,1,0:T(8,128)(2,1)} copy(bf16[32,2,24,2048]{3,2,0,1:T(8,128)(2,1)} %convert_bitcast_fusion) | data formatting | bytes 12582912 | tf_op jit(solution)/shard_map/convert_element_type | solution.py:185
  351.5 6.7 %all-to-all-start.1 = ((bf16[32,2,24,2048]{3,2,1,0:T(8,128)(2,1)}), bf16[32,2,24,2048]{3,2,1,0:T(8,128)(2,1)}, u32[]{:S(2)}, u32[]{:S(2)}) async-start(bf16[32,2,24,2048]{3,2,1,0:T(8,128)(2,1)} %copy.85), calls=%async_computation.1 | async-start | bytes 12582912 | tf_op jit(solution)/shard_map/all_to_all | solution.py:182
  358.5 2.4 reshape.278
  360.8 2.9 reshape.277
  363.8 2.5 copy.87
  366.8 132.8 %all-to-all-done.1 = bf16[32,2,24,2048]{3,2,1,0:T(8,128)(2,1)} async-done(((bf16[32,2,24,2048]{3,2,1,0:T(8,128)(2,1)}), bf16[32,2,24,2048]{3,2,1,0:T(8,128)(2,1)}, u32[]{:S(2)}, u32[]{:S(2)}) %all-to-all-start.1) | async-done | bytes 6291488 | tf_op jit(solution)/shard_map/all_to_all | solution.py:182
  499.6 12.4 %gather_fusion.1 = bf16[1024,2048]{1,0:T(8,128)(2,1)} fusion(bf16[1536,2048]{1,0:T(8,128)(2,1)} %bitcast.20, s32[1024]{0:T(1024)S(1)} %broadcast_clamp_fusion), kind=kCustom, calls=%fused_computation.1 | custom fusion | bytes 8392704 | tf_op jit(solution)/shard_map/gather | solution.py:192
  512.0 7.5 %fusion = bf16[128,2048]{1,0:T(8,128)(2,1)} fusion(bf16[1024,2048]{1,0:T(8,128)(2,1)} %gather_fusion.1, f32[128,8]{1,0:T(8,128)S(1)} %copy.86), kind=kLoop, calls=%fused_computation.4 | loop fusion | flops 6029312 | bytes 4722688 | tf_op jit(solution)/shard_map/reduce_sum | solution.py:193
  519.5 2.2 convolution_convert_fusion.2
  522.4 2.5 copy.88
  524.9 2.2 convolution_convert_fusion.1
  527.8 69.8 %all-reduce.6.cloned.1.call-done = bf16[128,2048]{1,0:T(8,128)(2,1)} async-done(((bf16[128,2048]{1,0:T(8,128)(2,1)}), bf16[128,2048]{1,0:T(8,128)(2,1)}) %all-reduce.6.cloned.1.call-update) | async-done | bytes 524304 | tf_op jit(solution)/shard_map/psum | solution.py:196
  597.6 2.4 add_convert_fusion
  (99 shorter events, 10.4 us)
Async XLA Ops:
  7.2 328.8 %copy-start = (bf16[2,128,2048]{2,1,0:T(8,128)(2,1)S(1)}, bf16[2,128,2048]{2,1,0:T(8,128)(2,1)}, u32[]{:S(2)}) copy-start(bf16[2,128,2048]{2,1,0:T(8,128)(2,1)} %param.27) | copy-start | bytes 3145732
  7.2 6.8 %copy-start.5 = (bf16[128,2048]{1,0:T(8,128)(2,1)S(1)}, bf16[128,2048]{1,0:T(8,128)(2,1)}, u32[]{:S(2)}) copy-start(bf16[128,2048]{1,0:T(8,128)(2,1)} %param.14) | copy-start | bytes 1572868
  7.2 6.8 %copy-start.20 = (f32[2048]{0:T(1024)S(1)}, f32[2048]{0:T(1024)}, u32[]{:S(2)}) copy-start(f32[2048]{0:T(1024)} %param.17) | copy-start | bytes 24580
  7.2 6.8 %copy-start.17 = (bf16[2048,256]{1,0:T(8,128)(2,1)S(1)}, bf16[2048,256]{1,0:T(8,128)(2,1)}, u32[]{:S(2)}) copy-start(bf16[2048,256]{1,0:T(8,128)(2,1)} %param.18) | copy-start | bytes 3145732
  7.2 72.2 %all-gather.2.cloned.1.call-start = ((), (), s32[]{:S(2)}) async-start(), calls=%async_computation.2 | async-start | bytes 4325376 | tf_op jit(solution)/shard_map/all_gather | solution.py:98
  10.4 5.6 copy-start.14
  16.0 155.9 %all-reduce.4.cloned.1.call-start = ((), (), s32[]{:S(2)}) async-start(), calls=%async_computation.3 | async-start | bytes 1048576 | tf_op jit(solution)/shard_map/psum | solution.py:147
  84.3 6.0 copy-start.2
  87.2 3.1 copy-start.10
  87.2 4.2 copy-start.11
  91.5 1.2 copy-start.12
  91.5 80.4 %copy-start.6 = (bf16[128,2048]{1,0:T(8,128)(2,1)S(1)}, bf16[128,2048]{1,0:T(8,128)(2,1)}, u32[]{:S(2)}) copy-start(bf16[128,2048]{1,0:T(8,128)(2,1)} %param.14) | copy-start | bytes 1572868
  91.5 81.7 %copy-start.15 = (f32[2048]{0:T(1024)S(1)}, f32[2048]{0:T(1024)}, u32[]{:S(2)}) copy-start(f32[2048]{0:T(1024)} %param.22) | copy-start | bytes 24580
  174.4 0.8 copy-start.8
  182.4 151.7 %copy-start.18 = (bf16[2,2048,128]{2,1,0:T(8,128)(2,1)S(1)}, bf16[2,2048,128]{2,1,0:T(8,128)(2,1)}, u32[]{:S(2)}) copy-start(bf16[2,2048,128]{2,1,0:T(8,128)(2,1)} %param.25) | copy-start | bytes 3145732
  331.4 2.7 copy-start.7
  334.0 1.9 copy-start.19
  351.5 7.0 %copy-start.3 = (bf16[4096,256]{1,0:T(8,128)(2,1)S(1)}, bf16[4096,256]{1,0:T(8,128)(2,1)}, u32[]{:S(2)}) copy-start(bf16[4096,256]{1,0:T(8,128)(2,1)} %copy-done.2) | copy-start | bytes 6291460
  351.5 148.1 %all-to-all-start.1 = ((bf16[32,2,24,2048]{3,2,1,0:T(8,128)(2,1)}), bf16[32,2,24,2048]{3,2,1,0:T(8,128)(2,1)}, u32[]{:S(2)}, u32[]{:S(2)}) async-start(bf16[32,2,24,2048]{3,2,1,0:T(8,128)(2,1)} %copy.85), calls=%async_computation.1 | async-start | bytes 12582912 | tf_op jit(solution)/shard_map/all_to_all | solution.py:182
  358.2 239.4 %all-reduce.6.cloned.1.call-start = ((), (), s32[]{:S(2)}) async-start(), calls=%async_computation.4 | async-start | bytes 1048576 | tf_op jit(solution)/shard_map/psum | solution.py:196
  360.8 5.5 copy-start.9
  360.8 5.5 copy-start.13
  512.0 7.5 %copy-start.16 = (s32[256]{0:T(256)S(1)}, s32[256]{0:T(256)}, u32[]{:S(2)}) copy-start(s32[256]{0:T(256)} %param.16) | copy-start | bytes 3076
  512.0 10.4 %copy-start.4 = (bf16[256,4096]{1,0:T(8,128)(2,1)S(1)}, bf16[256,4096]{1,0:T(8,128)(2,1)}, u32[]{:S(2)}) copy-start(bf16[256,4096]{1,0:T(8,128)(2,1)} %reshape.278) | copy-start | bytes 6291460
  522.4 77.6 %copy-start.1 = (bf16[2,128,2048]{2,1,0:T(8,128)(2,1)S(1)}, bf16[2,128,2048]{2,1,0:T(8,128)(2,1)}, u32[]{:S(2)}) copy-start(bf16[2,128,2048]{2,1,0:T(8,128)(2,1)} %param.27) | copy-start | bytes 3145732
Sparse Core Ops, SparseCore 0:
  16.1 63.2 all-gather.1
  94.0 77.8 all-reduce.3
  519.6 77.9 all-reduce.5
